TPU v7x, 256 devices: a whole 4x4x8 slice. The times are simulated.
256 devices in a mesh: gx: 8 (over z_lo, x), gy: 32 (over y, z_hi, core).
Axes of the slice: x: 4, y: 4, z: 8 (z_hi: 4, z_lo: 2; z = z_hi * 2 + z_lo), core: 2. Of those that a mesh axis runs over, the one named last changes fastest.
Arguments:
- offsets: float32 [3, 16, 64, 2, 128], P(None, 'gx', 'gy'), may hold values from 0 to 1
- velocity: float32 [3, 16, 64, 2, 128], P(None, 'gx', 'gy'), may hold values from -6 to 6
- mass: float32 [16, 64, 2, 128], P('gx', 'gy'), may hold values from 0.00390625 to 0.03125
- energy: float32 [16, 64, 2, 128], P('gx', 'gy'), may hold values from 0.3 to 3
- counts: int32 [16, 64, 2], P('gx', 'gy'), may hold values from 1 to 128
Outputs:
- density: float32 [16, 64, 2, 128], P('gx', 'gy')
- acceleration: float32 [3, 16, 64, 2, 128], P(None, 'gx', 'gy')
- heating: float32 [16, 64, 2, 128], P('gx', 'gy')
Inputs may be any that keep to these rules, and one draw needn't show every extreme that they name: Slots of a cell from counts on hold no particle.
All inputs are finite; a program needn't handle non-finite values.
Results may differ from a plain program's by a relative error of at most 0.0003.
Values sent between devices are 32-bit elements; how exact they have to be, the bound alone decides.
No kernel may reach another device: no remote copies, remote signals or barrier semaphores. Data moves between devices by JAX's collectives and lax.ppermute only.
A program may use at most 64 MiB of HBM per device.

v0:
```python
import math

import jax
import jax.numpy as jnp
from jax import lax
from jax.sharding import PartitionSpec as P

SMOOTHING = 0.5
NORMALISE = 1.0 / (math.pi * 0.125)
ADIABATIC = 5.0 / 3.0
VISC_ALPHA = 1.0
VISC_BETA = 2.0
SOFTENING = 0.01


def from_behind(block, axis, distance):
    devices = range(lax.axis_size(axis))
    route = [((i - distance) % len(devices), i) for i in devices]
    return lax.ppermute(block, axis, route)


def with_halo(cells, sides, width):
    for axis, dim in sides:
        count = lax.axis_size(axis)
        head = lax.slice_in_dim(cells, 0, width, axis=dim)
        tail = lax.slice_in_dim(cells, cells.shape[dim] - width, cells.shape[dim], axis=dim)
        cells = jnp.concatenate(
            [
                lax.ppermute(tail, axis, [(i, (i + 1) % count) for i in range(count)]),
                cells,
                lax.ppermute(head, axis, [((i + 1) % count, i) for i in range(count)]),
            ],
            axis=dim,
        )
    return cells


def offsets_list():
    result = []
    for shift_x in (-1, 0, 1):
        for shift_y in (-1, 0, 1):
            for shift_z in (-1, 0, 1):
                result.append((shift_x, shift_y, shift_z))
    return result


def forward_list():
    return [delta for delta in offsets_list() if delta > (0, 0, 0)]


def density_terms(own_cell, near_cell, delta):
    step = jnp.asarray(delta, jnp.float32).reshape(3, 1, 1, 1)
    separation = own_cell[0:3, :, :, None] - near_cell[0:3, :, None, :] - step
    scaled = jnp.sqrt(jnp.sum(separation * separation, axis=0)) / SMOOTHING
    outer = jnp.maximum(2.0 - scaled, 0.0)
    inner = jnp.maximum(1.0 - scaled, 0.0)
    kernel = NORMALISE * (0.25 * outer * outer * outer - inner * inner * inner)
    return jnp.sum(kernel * near_cell[6][:, None, :], axis=-1)


def density_pair(own_cell, near_cell, delta):
    step = jnp.asarray(delta, jnp.float32).reshape(3, 1, 1, 1)
    separation = own_cell[0:3, :, :, None] - near_cell[0:3, :, None, :] - step
    scaled = jnp.sqrt(jnp.sum(separation * separation, axis=0)) / SMOOTHING
    outer = jnp.maximum(2.0 - scaled, 0.0)
    inner = jnp.maximum(1.0 - scaled, 0.0)
    kernel = NORMALISE * (0.25 * outer * outer * outer - inner * inner * inner)
    to_own = jnp.sum(kernel * near_cell[6][:, None, :], axis=-1)
    to_near = jnp.sum(kernel * own_cell[6][:, :, None], axis=1)
    return (to_own[None], to_near[None])


def pair_common(own_cell, near_cell, delta):
    step = jnp.asarray(delta, jnp.float32).reshape(3, 1, 1, 1)
    separation = own_cell[0:3, :, :, None] - near_cell[0:3, :, None, :] - step
    relative = own_cell[3:6, :, :, None] - near_cell[3:6, :, None, :]
    distance_sq = jnp.sum(separation * separation, axis=0)
    scaled = jnp.sqrt(distance_sq) / SMOOTHING
    safe_scaled = jnp.where(scaled < 1.0, 1.0, scaled)
    outer = jnp.maximum(2.0 - scaled, 0.0)
    slope = jnp.where(scaled < 1.0, -3.0 + 2.25 * scaled, -0.75 * outer * outer / safe_scaled)
    base = NORMALISE / (SMOOTHING * SMOOTHING) * slope
    approach = jnp.sum(relative * separation, axis=0)
    closing = (
        SMOOTHING * jnp.minimum(approach, 0.0) / (distance_sq + SOFTENING * SMOOTHING * SMOOTHING)
    )
    sound = 0.5 * (own_cell[8][:, :, None] + near_cell[8][:, None, :])
    mean_rho = 0.5 * (own_cell[9][:, :, None] + near_cell[9][:, None, :])
    viscous = (-VISC_ALPHA * sound * closing + VISC_BETA * closing * closing) / mean_rho
    return (separation, base, approach, viscous)


def force_terms(own_cell, near_cell, delta):
    separation, base, approach, viscous = pair_common(own_cell, near_cell, delta)
    weight = near_cell[6][:, None, :] * base
    pushing = weight * (own_cell[7][:, :, None] + near_cell[7][:, None, :] + viscous)
    accel = -jnp.sum(pushing[None] * separation, axis=-1)
    heat = jnp.sum(weight * (own_cell[7][:, :, None] + 0.5 * viscous) * approach, axis=-1)
    return jnp.concatenate([accel, heat[None]], axis=0)


def force_pair(own_cell, near_cell, delta):
    separation, base, approach, viscous = pair_common(own_cell, near_cell, delta)
    pushing = base * (own_cell[7][:, :, None] + near_cell[7][:, None, :] + viscous)
    vector = pushing[None] * separation
    accel_own = -jnp.sum(vector * near_cell[6][None, :, None, :], axis=-1)
    accel_near = jnp.sum(vector * own_cell[6][None, :, :, None], axis=2)
    heat_own = jnp.sum(
        base * (own_cell[7][:, :, None] + 0.5 * viscous) * approach * near_cell[6][:, None, :],
        axis=-1,
    )
    heat_near = jnp.sum(
        base * (near_cell[7][:, None, :] + 0.5 * viscous) * approach * own_cell[6][:, :, None],
        axis=1,
    )
    to_own = jnp.concatenate([accel_own, heat_own[None]], axis=0)
    to_near = jnp.concatenate([accel_near, heat_near[None]], axis=0)
    return (to_own, to_near)


def half_apply(extended, count_x, count_y, self_terms, pair_terms, rows_out):
    layers = extended.shape[3] - 2
    slots = extended.shape[4]
    start = jnp.zeros((rows_out, count_x + 2, count_y + 2, layers + 2, slots), jnp.float32)

    def column(position, totals):
        first = position // count_y
        second = position % count_y
        zero = jnp.zeros((), jnp.int32)
        neighbours = lax.dynamic_slice(
            extended,
            (zero, first, second, zero, zero),
            (extended.shape[0], 3, 3, layers + 2, slots),
        )
        own_cell = neighbours[:, 1, 1, 1 : layers + 1]
        local = jnp.zeros((rows_out, 3, 3, layers + 2, slots), jnp.float32)
        own_part = self_terms(own_cell, own_cell, (0, 0, 0)).reshape(rows_out, layers, slots)
        for delta in forward_list():
            near_cell = neighbours[
                :, 1 + delta[0], 1 + delta[1], 1 + delta[2] : 1 + delta[2] + layers
            ]
            to_own, to_near = pair_terms(own_cell, near_cell, delta)
            own_part = own_part + to_own
            local = local.at[
                :, 1 + delta[0], 1 + delta[1], 1 + delta[2] : 1 + delta[2] + layers
            ].add(to_near)
        local = local.at[:, 1, 1, 1 : layers + 1].add(own_part)
        block = lax.dynamic_slice(
            totals, (zero, first, second, zero, zero), (rows_out, 3, 3, layers + 2, slots)
        )
        return lax.dynamic_update_slice(totals, block + local, (zero, first, second, zero, zero))

    totals = lax.fori_loop(0, count_x * count_y, column, start)
    return totals[:, :, :, 1 : layers + 1]


def fold_back(totals):
    lower = totals[:, :, 0]
    upper = totals[:, :, -1]
    from_above = from_behind(lower, "gy", -1)
    from_below = from_behind(upper, "gy", 1)
    middle = totals[:, :, 1:-1]
    middle = middle.at[:, :, -1].add(from_above)
    middle = middle.at[:, :, 0].add(from_below)
    from_left = from_behind(middle[:, -1], "gx", 1)
    owned = middle[:, 1:-1]
    return owned.at[:, 0].add(from_left)


def force_inputs(particles, density_safe):
    energy_part = particles[7]
    pressure_term = (ADIABATIC - 1.0) * energy_part / density_safe
    sound = jnp.sqrt(ADIABATIC * (ADIABATIC - 1.0) * energy_part)
    return jnp.concatenate(
        [particles[0:7], pressure_term[None], sound[None], density_safe[None]], axis=0
    )


def spread(particles, margin):
    return with_halo(particles, (("gx", 1), ("gy", 2)), margin)


def near_densities(density_safe):
    return with_halo(density_safe, (("gx", 0), ("gy", 1)), 1)


def shards(offsets, velocity, mass, energy, counts):
    slots = mass.shape[-1]
    count_x = mass.shape[0]
    count_y = mass.shape[1]
    occupied = (jnp.arange(slots, dtype=jnp.int32)[None, None, None, :] < counts[..., None]).astype(
        jnp.float32
    )
    particles = jnp.concatenate([offsets, velocity, (mass * occupied)[None], energy[None]], axis=0)
    particles = jnp.pad(particles, ((0, 0), (0, 0), (0, 0), (1, 1), (0, 0)))
    extended = spread(particles, 1)
    density = fold_back(half_apply(extended, count_x, count_y, density_terms, density_pair, 1))[0]
    density_safe = jnp.where(particles[6, :, :, 1:-1] > 0.0, density, 1.0)
    density_safe = jnp.pad(density_safe, ((0, 0), (0, 0), (1, 1), (0, 0)), constant_values=1.0)
    density_near = near_densities(density_safe)
    forces = fold_back(
        half_apply(
            force_inputs(extended, density_near), count_x, count_y, force_terms, force_pair, 4
        )
    )
    return (density * occupied, forces[0:3] * occupied[None], forces[3] * occupied)


def solution(mesh):
    in_specs = (
        P(None, "gx", "gy", None, None),
        P(None, "gx", "gy", None, None),
        P("gx", "gy", None, None),
        P("gx", "gy", None, None),
        P("gx", "gy", None),
    )
    out_specs = (
        P("gx", "gy", None, None),
        P(None, "gx", "gy", None, None),
        P("gx", "gy", None, None),
    )
    return jax.shard_map(shards, mesh=mesh, in_specs=in_specs, out_specs=out_specs, check_vma=False)
```

profile of v0, /device:TPU:38, one launch (start us, length us, event | category | flops | bytes accessed | tf_op | source)
XLA Modules:
  0.0 125.3 jit_solution(823278554128883389)
XLA Ops:
  0.6 0.8 fusion.223
  1.4 0.8 select_maximum_fusion.1
  2.2 1.8 %collective-permute-start = (f32[8,1,2,4,128]{4,3,2,1,0:T(4,128)S(1)}, f32[8,1,2,4,128]{4,3,2,1,0:T(4,128)S(1)}, u32[]{:S(2)}, u32[]{:S(2)}) collective-permute-start(f32[8,1,2,4,128]{4,3,2,1,0:T(4,128)S(1)} %get-tuple-element.2165), channel_id=1, source_target_pairs={{0,32},{32,64},{64,96},{96,128},{128,160},{160,192},{192,224},{224... | collective-permute-start | bytes 98312 | tf_op jit(solution)/shard_map/ppermute | solution.py:29
  4.3 1.9 %collective-permute-done = f32[8,1,2,4,128]{4,3,2,1,0:T(4,128)S(1)} collective-permute-done((f32[8,1,2,4,128]{4,3,2,1,0:T(4,128)S(1)}, f32[8,1,2,4,128]{4,3,2,1,0:T(4,128)S(1)}, u32[]{:S(2)}, u32[]{:S(2)}) %collective-permute-start) | collective-permute-done | bytes 32800 | tf_op jit(solution)/shard_map/ppermute | solution.py:29
  6.2 3.8 %collective-permute-done.1 = f32[8,1,2,4,128]{4,3,2,1,0:T(4,128)S(1)} collective-permute-done((f32[8,1,2,4,128]{4,3,2,1,0:T(4,128)S(1)}, f32[8,1,2,4,128]{4,3,2,1,0:T(4,128)S(1)}, u32[]{:S(2)}, u32[]{:S(2)}) %collective-permute-start.1) | collective-permute-done | bytes 32800 | tf_op jit(solution)/shard_map/ppermute | solution.py:31
  10.2 6.0 %collective-permute-start.3 = (f32[8,4,1,4,128]{4,3,2,1,0:T(4,128)S(1)}, f32[8,4,1,4,128]{4,3,2,1,0:T(4,128)S(1)}, u32[]{:S(2)}, u32[]{:S(2)}) collective-permute-start(f32[8,4,1,4,128]{4,3,2,1,0:T(4,128)S(1)} %get-tuple-element.2164), channel_id=1, source_target_pairs={{1,0},{2,1},{3,2},{4,3},{5,4},{6,5},{7,6},{8,7},{9,8},{10,9},{11,1... | collective-permute-start | bytes 196616 | tf_op jit(solution)/shard_map/ppermute | solution.py:31
  16.1 2.3 %collective-permute-done.2 = f32[8,4,1,4,128]{4,3,2,1,0:T(4,128)S(1)} collective-permute-done((f32[8,4,1,4,128]{4,3,2,1,0:T(4,128)S(1)}, f32[8,4,1,4,128]{4,3,2,1,0:T(4,128)S(1)}, u32[]{:S(2)}, u32[]{:S(2)}) %collective-permute-start.2) | collective-permute-done | bytes 65568 | tf_op jit(solution)/shard_map/ppermute | solution.py:29
  19.4 13.7 %while.68 = (s32[]{:T(128)}, f32[1,4,4,4,128]{4,3,2,1,0:T(4,128)S(1)}, f32[8,4,4,4,128]{4,3,2,1,0:T(4,128)S(1)}, s32[]{:T(128)}, s32[]{:T(128)}, /*index=5*/s32[...) while((s32[]{:T(128)}, ...), condition=%wide.region_42.43_spmd.clone, body=%wide.region_0.42_spmd.sunk.clone.sunk | while | flops 11771419 | bytes 4011732 | solution.py:153
  20.4 1.0 multiply_reduce_fusion.124
  23.8 1.0 multiply_reduce_fusion.124
  27.2 1.0 multiply_reduce_fusion.124
  30.7 1.0 multiply_reduce_fusion.124
  33.1 5.6 %collective-permute-start.4 = (f32[1,4,2,128]{3,2,1,0:T(2,128)S(1)}, f32[1,4,2,128]{3,2,1,0:T(2,128)S(1)}, u32[]{:S(2)}, u32[]{:S(2)}) collective-permute-start(f32[1,4,2,128]{3,2,1,0:T(2,128)S(1)} %get-tuple-element.2168), channel_id=1, source_target_pairs={{1,0},{2,1},{3,2},{4,3},{5,4},{6,5},{7,6},{8,7},{9,8},{10,9},{11,1... | collective-permute-start | bytes 12296 | tf_op jit(solution)/shard_map/ppermute | solution.py:19
  38.7 1.3 %collective-permute-done.4 = f32[1,4,2,128]{3,2,1,0:T(2,128)S(1)} collective-permute-done((f32[1,4,2,128]{3,2,1,0:T(2,128)S(1)}, f32[1,4,2,128]{3,2,1,0:T(2,128)S(1)}, u32[]{:S(2)}, u32[]{:S(2)}) %collective-permute-start.4) | collective-permute-done | bytes 4128 | tf_op jit(solution)/shard_map/ppermute | solution.py:19
  40.1 5.9 %collective-permute-done.5 = f32[1,4,2,128]{3,2,1,0:T(2,128)S(1)} collective-permute-done((f32[1,4,2,128]{3,2,1,0:T(2,128)S(1)}, f32[1,4,2,128]{3,2,1,0:T(2,128)S(1)}, u32[]{:S(2)}, u32[]{:S(2)}) %collective-permute-start.5) | collective-permute-done | bytes 4128 | tf_op jit(solution)/shard_map/ppermute | solution.py:19
  46.0 0.7 collective-permute-start.6
  46.7 3.0 %collective-permute-done.6 = f32[1,2,2,128]{3,2,1,0:T(2,128)S(1)} collective-permute-done((f32[1,2,2,128]{3,2,1,0:T(2,128)S(1)}, f32[1,2,2,128]{3,2,1,0:T(2,128)S(1)}, u32[]{:S(2)}, u32[]{:S(2)}) %collective-permute-start.6) | collective-permute-done | bytes 2080 | tf_op jit(solution)/shard_map/ppermute | solution.py:19
  50.4 2.7 %collective-permute-start.7 = (f32[1,2,4,128]{3,2,1,0:T(4,128)S(1)}, f32[1,2,4,128]{3,2,1,0:T(4,128)S(1)}, u32[]{:S(2)}, u32[]{:S(2)}) collective-permute-start(f32[1,2,4,128]{3,2,1,0:T(4,128)S(1)} %get-tuple-element.2175), channel_id=1, source_target_pairs={{0,32},{32,64},{64,96},{96,128},{128,160},{160,192},{192,224},{224... | collective-permute-start | bytes 12296 | tf_op jit(solution)/shard_map/ppermute | solution.py:29
  53.1 1.3 %collective-permute-done.7 = f32[1,2,4,128]{3,2,1,0:T(4,128)S(1)} collective-permute-done((f32[1,2,4,128]{3,2,1,0:T(4,128)S(1)}, f32[1,2,4,128]{3,2,1,0:T(4,128)S(1)}, u32[]{:S(2)}, u32[]{:S(2)}) %collective-permute-start.7) | collective-permute-done | bytes 4128 | tf_op jit(solution)/shard_map/ppermute | solution.py:29
  54.4 4.4 %collective-permute-done.8 = f32[1,2,4,128]{3,2,1,0:T(4,128)S(1)} collective-permute-done((f32[1,2,4,128]{3,2,1,0:T(4,128)S(1)}, f32[1,2,4,128]{3,2,1,0:T(4,128)S(1)}, u32[]{:S(2)}, u32[]{:S(2)}) %collective-permute-start.8) | collective-permute-done | bytes 4128 | tf_op jit(solution)/shard_map/ppermute | solution.py:31
  58.9 6.0 %collective-permute-start.10 = (f32[4,1,4,128]{3,2,1,0:T(4,128)S(1)}, f32[4,1,4,128]{3,2,1,0:T(4,128)S(1)}, u32[]{:S(2)}, u32[]{:S(2)}) collective-permute-start(f32[4,1,4,128]{3,2,1,0:T(4,128)S(1)} %get-tuple-element.2172), channel_id=1, source_target_pairs={{1,0},{2,1},{3,2},{4,3},{5,4},{6,5},{7,6},{8,7},{9,8},{10,9},{11,1... | collective-permute-start | bytes 24584 | tf_op jit(solution)/shard_map/ppermute | solution.py:31
  64.9 1.3 %collective-permute-done.9 = f32[4,1,4,128]{3,2,1,0:T(4,128)S(1)} collective-permute-done((f32[4,1,4,128]{3,2,1,0:T(4,128)S(1)}, f32[4,1,4,128]{3,2,1,0:T(4,128)S(1)}, u32[]{:S(2)}, u32[]{:S(2)}) %collective-permute-start.9) | collective-permute-done | bytes 8224 | tf_op jit(solution)/shard_map/ppermute | solution.py:29
  66.4 40.3 %while.69 = (s32[]{:T(128)}, f32[4,4,4,4,128]{4,3,0,2,1:T(4,128)S(1)}, f32[10,4,4,4,128]{4,3,2,1,0:T(4,128)S(1)}, s32[]{:T(128)}, s32[]{:T(128)}, /*index=5*/s32...) while((s32[]{:T(128)}, ...), condition=%wide.region_126.127_spmd.clone, body=%wide.region_43.126_spmd.sunk.clone.sunk | while | flops 37114656 | bytes 12823496 | solution.py:153
  66.8 0.7 multiply_reduce_fusion.125
  68.3 0.7 multiply_reduce_fusion.127
  70.1 0.8 multiply_reduce_fusion.128
  73.0 0.8 multiply_reduce_fusion.137
  73.8 0.8 multiply_reduce_fusion.135
  74.6 0.8 multiply_reduce_fusion.131
  76.9 0.7 multiply_reduce_fusion.125
  80.2 0.8 multiply_reduce_fusion.128
  83.1 0.8 multiply_reduce_fusion.137
  83.9 0.8 multiply_reduce_fusion.135
  84.7 0.8 multiply_reduce_fusion.131
  87.0 0.7 multiply_reduce_fusion.125
  90.3 0.8 multiply_reduce_fusion.128
  93.2 0.8 multiply_reduce_fusion.137
  94.0 0.8 multiply_reduce_fusion.135
  94.8 0.8 multiply_reduce_fusion.131
  97.1 0.7 multiply_reduce_fusion.125
  100.3 0.8 multiply_reduce_fusion.128
  103.3 0.8 multiply_reduce_fusion.137
  104.1 0.8 multiply_reduce_fusion.135
  104.9 0.8 multiply_reduce_fusion.131
  106.8 6.0 %collective-permute-start.11 = (f32[4,4,2,128]{3,2,0,1:T(2,128)S(1)}, f32[4,4,2,128]{3,2,0,1:T(2,128)S(1)}, u32[]{:S(2)}, u32[]{:S(2)}) collective-permute-start(f32[4,4,2,128]{3,2,0,1:T(2,128)S(1)} %get-tuple-element.2162), channel_id=1, source_target_pairs={{1,0},{2,1},{3,2},{4,3},{5,4},{6,5},{7,6},{8,7},{9,8},{10,9},{11,1... | collective-permute-start | bytes 49160 | tf_op jit(solution)/shard_map/ppermute | solution.py:19
  112.9 1.3 %collective-permute-done.11 = f32[4,4,2,128]{3,2,0,1:T(2,128)S(1)} collective-permute-done((f32[4,4,2,128]{3,2,0,1:T(2,128)S(1)}, f32[4,4,2,128]{3,2,0,1:T(2,128)S(1)}, u32[]{:S(2)}, u32[]{:S(2)}) %collective-permute-start.11) | collective-permute-done | bytes 16416 | tf_op jit(solution)/shard_map/ppermute | solution.py:19
  114.3 6.0 %collective-permute-done.12 = f32[4,4,2,128]{3,2,0,1:T(2,128)S(1)} collective-permute-done((f32[4,4,2,128]{3,2,0,1:T(2,128)S(1)}, f32[4,4,2,128]{3,2,0,1:T(2,128)S(1)}, u32[]{:S(2)}, u32[]{:S(2)}) %collective-permute-start.12) | collective-permute-done | bytes 16416 | tf_op jit(solution)/shard_map/ppermute | solution.py:19
  120.5 3.6 %collective-permute-done.13 = f32[4,2,2,128]{3,2,1,0:T(2,128)S(1)} collective-permute-done((f32[4,2,2,128]{3,2,1,0:T(2,128)S(1)}, f32[4,2,2,128]{3,2,1,0:T(2,128)S(1)}, u32[]{:S(2)}, u32[]{:S(2)}) %collective-permute-start.13) | collective-permute-done | bytes 8224 | tf_op jit(solution)/shard_map/ppermute | solution.py:19
  (328 shorter events, 36.2 us)
Async XLA Ops:
  0.6 0.8 copy-start.14
  2.2 4.0 %collective-permute-start = (f32[8,1,2,4,128]{4,3,2,1,0:T(4,128)S(1)}, f32[8,1,2,4,128]{4,3,2,1,0:T(4,128)S(1)}, u32[]{:S(2)}, u32[]{:S(2)}) collective-permute-start(f32[8,1,2,4,128]{4,3,2,1,0:T(4,128)S(1)} %get-tuple-element.2165), channel_id=1, source_target_pairs={{0,32},{32,64},{64,96},{96,128},{128,160},{160,192},{192,224},{224... | collective-permute-start | bytes 98312 | tf_op jit(solution)/shard_map/ppermute | solution.py:29
  4.0 6.0 %collective-permute-start.1 = (f32[8,1,2,4,128]{4,3,2,1,0:T(4,128)S(1)}, f32[8,1,2,4,128]{4,3,2,1,0:T(4,128)S(1)}, u32[]{:S(2)}, u32[]{:S(2)}) collective-permute-start(f32[8,1,2,4,128]{4,3,2,1,0:T(4,128)S(1)} %get-tuple-element.2166), channel_id=1, source_target_pairs={{32,0},{64,32},{96,64},{128,96},{160,128},{192,160},{224,192},{0,2... | collective-permute-start | bytes 98312 | tf_op jit(solution)/shard_map/ppermute | solution.py:31
  10.1 8.4 %collective-permute-start.2 = (f32[8,4,1,4,128]{4,3,2,1,0:T(4,128)S(1)}, f32[8,4,1,4,128]{4,3,2,1,0:T(4,128)S(1)}, u32[]{:S(2)}, u32[]{:S(2)}) collective-permute-start(f32[8,4,1,4,128]{4,3,2,1,0:T(4,128)S(1)} %get-tuple-element.2163), channel_id=1, source_target_pairs={{0,1},{1,2},{2,3},{3,4},{4,5},{5,6},{6,7},{7,8},{8,9},{9,10},{10,1... | collective-permute-start | bytes 196616 | tf_op jit(solution)/shard_map/ppermute | solution.py:29
  10.2 8.3 %collective-permute-start.3 = (f32[8,4,1,4,128]{4,3,2,1,0:T(4,128)S(1)}, f32[8,4,1,4,128]{4,3,2,1,0:T(4,128)S(1)}, u32[]{:S(2)}, u32[]{:S(2)}) collective-permute-start(f32[8,4,1,4,128]{4,3,2,1,0:T(4,128)S(1)} %get-tuple-element.2164), channel_id=1, source_target_pairs={{1,0},{2,1},{3,2},{4,3},{5,4},{6,5},{7,6},{8,7},{9,8},{10,9},{11,1... | collective-permute-start | bytes 196616 | tf_op jit(solution)/shard_map/ppermute | solution.py:31
  18.5 0.7 copy-start
  18.6 0.7 copy-start.1
  18.6 0.7 copy-start.2
  18.6 0.7 copy-start.3
  18.6 0.7 copy-start.4
  18.6 0.7 copy-start.5
  18.6 0.7 copy-start.6
  18.6 0.7 copy-start.7
  18.6 0.7 copy-start.8
  18.7 0.7 copy-start.9
  18.7 0.7 copy-start.10
  18.7 0.7 copy-start.11
  33.1 7.0 %collective-permute-start.4 = (f32[1,4,2,128]{3,2,1,0:T(2,128)S(1)}, f32[1,4,2,128]{3,2,1,0:T(2,128)S(1)}, u32[]{:S(2)}, u32[]{:S(2)}) collective-permute-start(f32[1,4,2,128]{3,2,1,0:T(2,128)S(1)} %get-tuple-element.2168), channel_id=1, source_target_pairs={{1,0},{2,1},{3,2},{4,3},{5,4},{6,5},{7,6},{8,7},{9,8},{10,9},{11,1... | collective-permute-start | bytes 12296 | tf_op jit(solution)/shard_map/ppermute | solution.py:19
  38.7 7.3 %collective-permute-start.5 = (f32[1,4,2,128]{3,2,1,0:T(2,128)S(1)}, f32[1,4,2,128]{3,2,1,0:T(2,128)S(1)}, u32[]{:S(2)}, u32[]{:S(2)}) collective-permute-start(f32[1,4,2,128]{3,2,1,0:T(2,128)S(1)} %get-tuple-element.2167), channel_id=1, source_target_pairs={{31,0},{0,1},{1,2},{2,3},{3,4},{4,5},{5,6},{6,7},{7,8},{8,9},{9,10... | collective-permute-start | bytes 12296 | tf_op jit(solution)/shard_map/ppermute | solution.py:19
  46.0 3.7 %collective-permute-start.6 = (f32[1,2,2,128]{3,2,1,0:T(2,128)S(1)}, f32[1,2,2,128]{3,2,1,0:T(2,128)S(1)}, u32[]{:S(2)}, u32[]{:S(2)}) collective-permute-start(f32[1,2,2,128]{3,2,1,0:T(2,128)S(1)} %slice_bitcast_fusion.8), channel_id=1, source_target_pairs={{224,0},{0,32},{32,64},{64,96},{96,128},{128,160},{160,192},{192,2... | collective-permute-start | bytes 6152 | tf_op jit(solution)/shard_map/ppermute | solution.py:19
  46.7 3.0 %copy-start.12 = (s32[2,2,2]{2,1,0:T(2,128)S(1)}, s32[2,2,2]{2,1,0:T(2,128)}, u32[]{:S(2)}) copy-start(s32[2,2,2]{2,1,0:T(2,128)} %param.109) | copy-start | bytes 100
  46.7 3.0 %copy-start.13 = (f32[2,2,2,128]{3,2,1,0:T(2,128)S(1)}, f32[2,2,2,128]{3,2,1,0:T(2,128)}, u32[]{:S(2)}) copy-start(f32[2,2,2,128]{3,2,1,0:T(2,128)} %param.107) | copy-start | bytes 12292
  50.4 4.1 %collective-permute-start.7 = (f32[1,2,4,128]{3,2,1,0:T(4,128)S(1)}, f32[1,2,4,128]{3,2,1,0:T(4,128)S(1)}, u32[]{:S(2)}, u32[]{:S(2)}) collective-permute-start(f32[1,2,4,128]{3,2,1,0:T(4,128)S(1)} %get-tuple-element.2175), channel_id=1, source_target_pairs={{0,32},{32,64},{64,96},{96,128},{128,160},{160,192},{192,224},{224... | collective-permute-start | bytes 12296 | tf_op jit(solution)/shard_map/ppermute | solution.py:29
  53.1 5.7 %collective-permute-start.8 = (f32[1,2,4,128]{3,2,1,0:T(4,128)S(1)}, f32[1,2,4,128]{3,2,1,0:T(4,128)S(1)}, u32[]{:S(2)}, u32[]{:S(2)}) collective-permute-start(f32[1,2,4,128]{3,2,1,0:T(4,128)S(1)} %get-tuple-element.2176), channel_id=1, source_target_pairs={{32,0},{64,32},{96,64},{128,96},{160,128},{192,160},{224,192},{0,2... | collective-permute-start | bytes 12296 | tf_op jit(solution)/shard_map/ppermute | solution.py:31
  58.8 7.4 %collective-permute-start.9 = (f32[4,1,4,128]{3,2,1,0:T(4,128)S(1)}, f32[4,1,4,128]{3,2,1,0:T(4,128)S(1)}, u32[]{:S(2)}, u32[]{:S(2)}) collective-permute-start(f32[4,1,4,128]{3,2,1,0:T(4,128)S(1)} %get-tuple-element.2171), channel_id=1, source_target_pairs={{0,1},{1,2},{2,3},{3,4},{4,5},{5,6},{6,7},{7,8},{8,9},{9,10},{10,1... | collective-permute-start | bytes 24584 | tf_op jit(solution)/shard_map/ppermute | solution.py:29
  58.9 7.3 %collective-permute-start.10 = (f32[4,1,4,128]{3,2,1,0:T(4,128)S(1)}, f32[4,1,4,128]{3,2,1,0:T(4,128)S(1)}, u32[]{:S(2)}, u32[]{:S(2)}) collective-permute-start(f32[4,1,4,128]{3,2,1,0:T(4,128)S(1)} %get-tuple-element.2172), channel_id=1, source_target_pairs={{1,0},{2,1},{3,2},{4,3},{5,4},{6,5},{7,6},{8,7},{9,8},{10,9},{11,1... | collective-permute-start | bytes 24584 | tf_op jit(solution)/shard_map/ppermute | solution.py:31
  106.8 7.4 %collective-permute-start.11 = (f32[4,4,2,128]{3,2,0,1:T(2,128)S(1)}, f32[4,4,2,128]{3,2,0,1:T(2,128)S(1)}, u32[]{:S(2)}, u32[]{:S(2)}) collective-permute-start(f32[4,4,2,128]{3,2,0,1:T(2,128)S(1)} %get-tuple-element.2162), channel_id=1, source_target_pairs={{1,0},{2,1},{3,2},{4,3},{5,4},{6,5},{7,6},{8,7},{9,8},{10,9},{11,1... | collective-permute-start | bytes 49160 | tf_op jit(solution)/shard_map/ppermute | solution.py:19
  112.8 7.5 %collective-permute-start.12 = (f32[4,4,2,128]{3,2,0,1:T(2,128)S(1)}, f32[4,4,2,128]{3,2,0,1:T(2,128)S(1)}, u32[]{:S(2)}, u32[]{:S(2)}) collective-permute-start(f32[4,4,2,128]{3,2,0,1:T(2,128)S(1)} %get-tuple-element.2161), channel_id=1, source_target_pairs={{31,0},{0,1},{1,2},{2,3},{3,4},{4,5},{5,6},{6,7},{7,8},{8,9},{9,10... | collective-permute-start | bytes 49160 | tf_op jit(solution)/shard_map/ppermute | solution.py:19
  120.3 3.7 %collective-permute-start.13 = (f32[4,2,2,128]{3,2,1,0:T(2,128)S(1)}, f32[4,2,2,128]{3,2,1,0:T(2,128)S(1)}, u32[]{:S(2)}, u32[]{:S(2)}) collective-permute-start(f32[4,2,2,128]{3,2,1,0:T(2,128)S(1)} %slice_bitcast_fusion.2), channel_id=1, source_target_pairs={{224,0},{0,32},{32,64},{64,96},{96,128},{128,160},{160,192},{192,2... | collective-permute-start | bytes 24584 | tf_op jit(solution)/shard_map/ppermute | solution.py:19
where the time goes:
time: 126 us; the launch traced here: 125 us
  other arithmetic  49.5 us (39%)
  waiting for transfers between devices  36.2 us (29%)
  starting transfers between devices  29.4 us (23%)
  local copies, waits for them, and re-layouts  7.68 us (6%)
  loops' own time  1.64 us (1%)
    ppermute x6, waiting for transfers between devices, from_behind(): return lax.ppermute(block, axis, route)  21.1 us
    reduce_sum x28, other arithmetic, force_pair(): jnp.sum(base * (own_cell[7][:, :, None] + 0.5 * viscous) * approach * nea...  15.6 us
    ppermute x6, starting transfers between devices, from_behind(): return lax.ppermute(block, axis, route)  12.5 us
    ppermute x4, starting transfers between devices, with_halo(): lax.ppermute(head, axis, [((i + 1) % count, i) for i in range(count)])  12.2 us
    reduce_sum x16, other arithmetic, force_pair(): accel_own = -jnp.sum(vector * near_cell[6][None, :, None, :], axis=-1)  11.8 us
    ppermute x4, waiting for transfers between devices, with_halo(): lax.ppermute(head, axis, [((i + 1) % count, i) for i in range(count)])  8.27 us
    ppermute x4, waiting for transfers between devices, with_halo(): lax.ppermute(tail, axis, [(i, (i + 1) % count) for i in range(count)])  6.85 us
    reduce_sum x8, other arithmetic, density_pair(): to_own = jnp.sum(kernel * near_cell[6][:, None, :], axis=-1)  6.13 us
  transfers between devices with their start and end apart: 14, of which 12 were waited for; matrix products, arithmetic and copies ran while one was open for 0% of the time, Pallas kernels for 0%

commit v1 on v0

v1 whole, which is shorter than its diff:
```python
import functools
import math

import jax
import jax.numpy as jnp
from jax import lax
from jax.experimental import pallas as pl
from jax.experimental.pallas import tpu as pltpu
from jax.sharding import PartitionSpec as P

F = jnp.float32
SIGMA = 8.0 / math.pi
DENS_UNROLL = 8
FORCE_UNROLL = 4
CHUNK = 32
GROUPS = 16 * 2 * 16 + 4 * 8 + 2 * CHUNK
TARGETS = [(a, b) for a in (0, 1) for b in (0, 1)]


def cell_id(r, s, z):
    return (r * 4 + s) * 2 + z


def place(e_ref, c, tile, r, s, z):
    row = lax.broadcasted_iota(jnp.int32, (8, 128), 0)
    base = jnp.where(row == 0, F(r - 2), jnp.where(row == 1, F(s - 2), F(z - 1)))
    e_ref[c] = jnp.where(row < 3, 2.0 * (tile + base), tile)


def cell_counts(e_ref):
    masses = e_ref[:, 6, :]
    filled = jnp.sum(jnp.where(masses > 0.0, 1.0, 0.0), axis=1, keepdims=True)
    groups = lax.shift_right_logical(filled.astype(jnp.int32) + 7, 3)
    return [groups[c, 0] for c in range(32)]


def pad_tile(values):
    lane = lax.broadcasted_iota(jnp.int32, (8, len(values)), 1)
    tile = jnp.zeros((8, len(values)), F)
    for k, value in enumerate(values):
        if value:
            tile = jnp.where(lane == k, F(value), tile)
    return tile


def pack(groups, tile_of, t_ref, unroll, pad):
    width = pad.shape[1]
    starts = []
    base = jnp.int32(0)
    for r in range(4):
        row = []
        for s in range(4):
            row.append(base)
            for z in range(2):
                c = cell_id(r, s, z)
                turned = tile_of(c).T
                for g in range(16):
                    t_ref[base + g, :, 0:width] = turned[8 * g : 8 * g + 8, :]
                base = base + groups[c]
        row.append(base)
        for g in range(unroll - 1):
            t_ref[base + g, :, 0:width] = pad
        base = base + (unroll - 1)
        starts.append(row)
    return starts, base


def spread(t_ref, j_ref, total, attrs):
    def body(i, carry):
        for n, k in enumerate(attrs):
            for g in range(CHUNK):
                at = i * CHUNK + g
                j_ref[n, at] = jnp.broadcast_to(t_ref[at, :, k : k + 1], (8, 128))
        return carry

    lax.fori_loop(0, (total + CHUNK - 1) // CHUNK, body, 0)


def density_kernel(own_ref, up_ref, right_ref, rho_ref, e_ref, t_ref, j_ref):
    for r in range(4):
        for s in range(4):
            for z in range(2):
                if r >= 2:
                    tile = right_ref[r - 2, s, z]
                elif s >= 2:
                    tile = up_ref[r, s - 2, z]
                else:
                    tile = own_ref[r, s, z]
                place(e_ref, cell_id(r, s, z), tile, r, s, z)
    groups = cell_counts(e_ref)
    starts, total = pack(
        groups, lambda c: e_ref[c], t_ref, DENS_UNROLL, pad_tile((1e3, 1e3, 1e3, 0, 0, 0, 0, 0))
    )
    spread(t_ref, j_ref, total, (0, 1, 2, 6))
    for n, (a, b) in enumerate(TARGETS):
        own = [cell_id(1 + a, 1 + b, z) for z in (0, 1)]
        mine = [[jnp.broadcast_to(e_ref[o, k : k + 1], (8, 128)) for k in range(3)] for o in own]
        sums = (jnp.zeros((8, 128), F), jnp.zeros((8, 128), F))
        for r in range(a, a + 3):
            low = starts[r][b]
            trips = (starts[r][b + 3] - low + (DENS_UNROLL - 1)) // DENS_UNROLL

            def body(t, sums, low=low, mine=mine):
                sums = list(sums)
                for u in range(DENS_UNROLL):
                    g = low + t * DENS_UNROLL + u
                    other = [j_ref[k, g] for k in range(4)]
                    for z in (0, 1):
                        dx, dy, dz = [mine[z][k] - other[k] for k in range(3)]
                        d2 = dx * dx + dy * dy + dz * dz
                        q = d2 * lax.rsqrt(jnp.maximum(d2, 1e-30))
                        outer = jnp.maximum(2.0 - q, 0.0)
                        inner = jnp.maximum(1.0 - q, 0.0)
                        w = 0.25 * (outer * outer * outer) - inner * inner * inner
                        sums[z] = sums[z] + w * other[3]
                return tuple(sums)

            sums = lax.fori_loop(0, trips, body, sums)
        for z in (0, 1):
            rho = jnp.sum(sums[z], axis=0, keepdims=True) * SIGMA
            rho = jnp.where(e_ref[own[z], 6:7] > 0.0, rho, 1.0)
            rho_ref[2 * n + z : 2 * n + z + 1, :] = rho


def force_kernel(
    own_ref, up_ref, right_ref, rho_ref, down_ref, left_ref,
    dens_ref, acc_ref, heat_ref, e_ref, f_ref, c_ref, t_ref, j_ref,
):
    for r in range(4):
        for s in range(4):
            for z in range(2):
                if r == 0:
                    tile = left_ref[2 * s + z]
                elif s == 0:
                    tile = down_ref[2 * (r - 1) + z]
                elif r == 3:
                    tile = right_ref[0, s - 1, z]
                elif s == 3:
                    tile = up_ref[r - 1, 0, z]
                else:
                    tile = own_ref[r - 1, s - 1, z]
                place(e_ref, cell_id(r, s, z), tile, r, s, z)
    for a, b in TARGETS:
        n = 2 * (2 * a + b)
        for source, r, s in (
            (rho_ref[n : n + 2], 2 + a, 2 + b),
            (down_ref[6, n : n + 2], 2 + a, b),
            (left_ref[8, n : n + 2], a, 2 + b),
            (left_ref[9, n : n + 2], a, b),
        ):
            c = cell_id(r, s, 0)
            f_ref[c : c + 2, :] = source
    energy = e_ref[:, 7, :]
    rho = f_ref[...]
    c_ref[0] = (2.0 / 3.0) * energy / rho
    c_ref[1] = 0.25 * jnp.sqrt((10.0 / 9.0) * energy)
    c_ref[2] = 0.25 * rho

    def tile_of(c):
        rows = [e_ref[c]] + [c_ref[k, c : c + 1, :] for k in range(3)] + [jnp.zeros((5, 128), F)]
        return jnp.concatenate(rows, axis=0)

    groups = cell_counts(e_ref)
    starts, total = pack(
        groups, tile_of, t_ref, FORCE_UNROLL,
        pad_tile((1e3, 1e3, 1e3, 0, 0, 0, 0, 0, 0, 0, 0.25, 0, 0, 0, 0, 0)),
    )
    spread(t_ref, j_ref, total, (0, 1, 2, 3, 4, 5, 6, 8, 9, 10))
    for a, b in TARGETS:
        own = [cell_id(1 + a, 1 + b, z) for z in (0, 1)]
        mine = [
            [jnp.broadcast_to(e_ref[o, k : k + 1], (8, 128)) for k in range(6)]
            + [jnp.broadcast_to(c_ref[k, o : o + 1, :], (8, 128)) for k in range(3)]
            for o in own
        ]
        sums = tuple(jnp.zeros((8, 128), F) for _ in range(10))
        for r in range(a, a + 3):
            low = starts[r][b]
            trips = (starts[r][b + 3] - low + (FORCE_UNROLL - 1)) // FORCE_UNROLL

            def body(t, sums, low=low, mine=mine):
                sums = list(sums)
                for u in range(FORCE_UNROLL):
                    g = low + t * FORCE_UNROLL + u
                    J = [j_ref[k, g] for k in range(10)]
                    for z in (0, 1):
                        I = mine[z]
                        dx, dy, dz = [I[k] - J[k] for k in range(3)]
                        d2 = dx * dx + dy * dy + dz * dz
                        vx = (I[3] - J[3]) * dx + (I[4] - J[4]) * dy + (I[5] - J[5]) * dz
                        rs = lax.rsqrt(jnp.maximum(d2, 1e-30))
                        q = d2 * rs
                        outer = jnp.maximum(2.0 - q, 0.0)
                        slope = jnp.where(q < 1.0, 4.0 - 3.0 * q, outer * outer * rs)
                        weight = slope * J[6]
                        closing = jnp.minimum(vx, 0.0)
                        soft = d2 + 0.01
                        visc = (
                            closing * (closing - (I[7] + J[8]) * soft)
                            / (soft * soft * (I[8] + J[9]))
                        )
                        push = weight * (I[6] + J[7] + visc)
                        sums[5 * z] += push * dx
                        sums[5 * z + 1] += push * dy
                        sums[5 * z + 2] += push * dz
                        work = weight * vx
                        sums[5 * z + 3] += work
                        sums[5 * z + 4] += work * visc
                return tuple(sums)

            sums = lax.fori_loop(0, trips, body, sums)
        for z in (0, 1):
            c = own[z]
            filled = jnp.where(e_ref[c, 6:7] > 0.0, 1.0, 0.0)
            scale = filled * (1.5 * SIGMA)
            s = [jnp.sum(sums[5 * z + k], axis=0, keepdims=True) * scale for k in range(5)]
            for k in range(3):
                acc_ref[k, a, b, z : z + 1, :] = s[k]
            heat_ref[a, b, z : z + 1, :] = -(c_ref[0, c : c + 1, :] * s[3] + 0.5 * s[4])
            dens_ref[a, b, z : z + 1, :] = f_ref[c : c + 1, :] * filled


VMEM = pl.BlockSpec(memory_space=pltpu.VMEM)


def shift(block, axis, step):
    count = lax.axis_size(axis)
    return lax.ppermute(block, axis, [((i + step) % count, i) for i in range(count)])


def shards(offsets, velocity, mass, energy, counts):
    slot = lax.broadcasted_iota(jnp.int32, (1, 1, 1, 128), 3)
    filled = (slot < counts[..., None]).astype(F)
    own = jnp.concatenate([offsets, velocity, (mass * filled)[None], energy[None]], axis=0)
    own = jnp.moveaxis(own, 0, 3)
    up = shift(own, "gy", 1)
    right = shift(jnp.concatenate([own, up], axis=1), "gx", 1)
    rho = pl.pallas_call(
        density_kernel,
        name="density",
        out_shape=jax.ShapeDtypeStruct((8, 128), F),
        in_specs=[VMEM] * 3,
        out_specs=VMEM,
        scratch_shapes=[
            pltpu.VMEM((32, 8, 128), F),
            pltpu.VMEM((GROUPS, 8, 128), F),
            pltpu.VMEM((4, GROUPS, 8, 128), F),
        ],
    )(own, up, right)
    cols = [own[0, 1], own[1, 1], right[0, 1], rho[None]]
    down = shift(jnp.concatenate(cols, axis=0), "gy", -1)
    cols = [down[2:4], own[1].reshape(4, 8, 128), up[1, 0], rho[None], down[6:7]]
    left = shift(jnp.concatenate(cols, axis=0), "gx", -1)
    return pl.pallas_call(
        force_kernel,
        name="force",
        out_shape=(
            jax.ShapeDtypeStruct((2, 2, 2, 128), F),
            jax.ShapeDtypeStruct((3, 2, 2, 2, 128), F),
            jax.ShapeDtypeStruct((2, 2, 2, 128), F),
        ),
        in_specs=[VMEM] * 6,
        out_specs=(VMEM, VMEM, VMEM),
        scratch_shapes=[
            pltpu.VMEM((32, 8, 128), F),
            pltpu.VMEM((32, 128), F),
            pltpu.VMEM((3, 32, 128), F),
            pltpu.VMEM((GROUPS, 8, 128), F),
            pltpu.VMEM((10, GROUPS, 8, 128), F),
        ],
    )(own, up, right, rho, down, left)


def solution(mesh):
    in_specs = (
        P(None, "gx", "gy", None, None),
        P(None, "gx", "gy", None, None),
        P("gx", "gy", None, None),
        P("gx", "gy", None, None),
        P("gx", "gy", None),
    )
    out_specs = (
        P("gx", "gy", None, None),
        P(None, "gx", "gy", None, None),
        P("gx", "gy", None, None),
    )
    return jax.shard_map(shards, mesh=mesh, in_specs=in_specs, out_specs=out_specs, check_vma=False)
```

time: 126 us -> 61.1 us (0.48)
  other arithmetic: 49.5 us -> 0.1 us
  Pallas kernels: 0 us -> 27.2 us
  starting transfers between devices: 29.4 us -> 8.28 us
  waiting for transfers between devices: 36.2 us -> 18 us
  local copies, waits for them, and re-layouts: 7.68 us -> 5.95 us
  loops' own time: 1.64 us -> 0 us
    reduce_sum x68 -> x0, other arithmetic: 43.1 us -> none  [the longest x28 15.6 us: force_pair(): jnp.sum(base * (own_cell[7][:, :, None] + 0.5 * viscous) * approach * nea...]
    pallas_call x0 -> x2, Pallas kernels: none -> 27.2 us  [the longest x1 17.3 us: shards(): pl.pallas_call(force_kernel, name='force', out_shape=(jax.ShapeDtypeStruc...]
    ppermute x14 -> x4, starting transfers between devices: 29.4 us -> 8.28 us  [shift(): lax.ppermute(block, axis, [((i + step) % count, i) for i in range(count)])]
    ppermute x14 -> x4, waiting for transfers between devices: 36.2 us -> 18 us  [shift(): lax.ppermute(block, axis, [((i + step) % count, i) for i in range(count)])]
    scatter-add x48 -> x0, local copies, waits for them, and re-layouts: 5.14 us -> none  [the longest x40 4.12 us: column(): local = local.at[:, 1 + delta[0], 1 + delta[1], 1 + delta[2]:1 + delta[2]...]
    unnamed x30 -> x28, local copies, waits for them, and re-layouts: 0.73 us -> 5.24 us
    mul x14 -> x1, other arithmetic: 2.18 us -> 0.07 us  [shards(): mass * filled]
    another operation x2 -> x0, loops' own time: 1.64 us -> none  [half_apply(): totals = lax.fori_loop(0, count_x * count_y, column, start)]
  transfers between devices with their start and end apart: 14 -> 4, of which waited for: 12 -> 4; matrix products, arithmetic and copies ran while one was open for 0% -> 0% of each run, Pallas kernels for 0% -> 0%
where the time goes in v1:
time: 61.1 us; the launch traced here: 60.2 us
  Pallas kernels  27.2 us (45%)
  waiting for transfers between devices  18 us (29%)
  starting transfers between devices  8.28 us (14%)
  local copies, waits for them, and re-layouts  5.95 us (10%)
  between operations  0.7 us (1%)
    ppermute x4, waiting for transfers between devices, shift(): lax.ppermute(block, axis, [((i + step) % count, i) for i in range(count)])  18 us
    pallas_call x1, Pallas kernels, shards(): pl.pallas_call(force_kernel, name='force', out_shape=(jax.ShapeDtypeStruc...  17.3 us
    pallas_call x1, Pallas kernels, shards(): pl.pallas_call(density_kernel, name='density', out_shape=jax.ShapeDtypeSt...  9.95 us
    ppermute x4, starting transfers between devices, shift(): lax.ppermute(block, axis, [((i + step) % count, i) for i in range(count)])  8.28 us
    unnamed x28, local copies, waits for them, and re-layouts  5.24 us
  transfers between devices with their start and end apart: 4, of which 4 were waited for; matrix products, arithmetic and copies ran while one was open for 0% of the time, Pallas kernels for 0%

profile of v1, /device:TPU:38, one launch (start us, length us, event | category | flops | bytes accessed | tf_op | source)
XLA Modules:
  0.0 60.2 jit_solution(17901117077245488014)
XLA Ops:
  0.6 0.0 copy-start.7
  0.6 0.7 %copy.8 = f32[3,2,2,2,128]{4,0,3,2,1:T(4,128)S(1)} copy(f32[3,2,2,2,128]{4,3,2,1,0:T(2,128)} %param.5) | data formatting | bytes 24576 | tf_op args[0]
  1.4 0.0 copy-done.7
  1.4 0.0 copy-start.9
  1.4 0.0 copy-start.10
  1.4 0.7 %copy-done.9 = f32[2,2,2,128]{3,2,1,0:T(2,128)S(1)} copy-done((f32[2,2,2,128]{3,2,1,0:T(2,128)S(1)}, f32[2,2,2,128]{3,2,1,0:T(2,128)}, u32[]{:S(2)}) %copy-start.9) | copy-done | bytes 4120
  2.0 0.0 copy-done.10
  2.1 0.0 copy-start.8
  2.1 0.1 compare_select_fusion
  2.1 0.6 %copy-done.8 = f32[2,2,2,128]{3,2,1,0:T(2,128)S(1)} copy-done((f32[2,2,2,128]{3,2,1,0:T(2,128)S(1)}, f32[2,2,2,128]{3,2,1,0:T(2,128)}, u32[]{:S(2)}) %copy-start.8) | copy-done | bytes 4120
  2.8 0.0 copy-start
  2.8 7.4 %collective-permute-start = (f32[2,2,2,8,128]{4,3,2,1,0:T(8,128)S(1)}, f32[2,2,2,8,128]{4,3,2,1,0:T(8,128)S(1)}, u32[]{:S(2)}, u32[]{:S(2)}) collective-permute-start(f32[2,2,2,8,128]{4,3,2,1,0:T(8,128)S(1)} %maximum_bitcast_fusion.own_ref), channel_id=1, source_target_pairs={{1,0},{2,1},{3,2},{4,3},{5,4},{6,5},{7,6},{8,7},{9,8},{10,9},{11,1... | collective-permute-start | bytes 98312 | tf_op jit(solution)/shard_map/ppermute | solution.py:228
  10.1 1.6 %collective-permute-done.up_ref = f32[2,2,2,8,128]{4,3,2,1,0:T(8,128)S(1)} collective-permute-done((f32[2,2,2,8,128]{4,3,2,1,0:T(8,128)S(1)}, f32[2,2,2,8,128]{4,3,2,1,0:T(8,128)S(1)}, u32[]{:S(2)}, u32[]{:S(2)}) %collective-permute-start) | collective-permute-done | bytes 32800 | tf_op jit(solution)/shard_map/ppermute | solution.py:228
  11.7 0.0 copy-start.2
  11.8 0.6 %copy-done.2 = f32[2,2,2,8,128]{4,3,2,1,0:T(8,128)} copy-done((f32[2,2,2,8,128]{4,3,2,1,0:T(8,128)}, f32[2,2,2,8,128]{4,3,2,1,0:T(8,128)S(1)}, u32[]{:S(2)}) %copy-start.2) | copy-done | bytes 32792
  12.4 0.8 %collective-permute-start.1 = (f32[2,4,2,8,128]{4,3,2,1,0:T(8,128)S(1)}, f32[2,4,2,8,128]{4,3,2,1,0:T(8,128)S(1)}, u32[]{:S(2)}, u32[]{:S(2)}) collective-permute-start(f32[2,4,2,8,128]{4,3,2,1,0:T(8,128)S(1)} %pad_maximum_fusion), channel_id=1, source_target_pairs={{32,0},{64,32},{96,64},{128,96},{160,128},{192,160},{224,192},{0,2... | collective-permute-start | bytes 196616 | tf_op jit(solution)/shard_map/ppermute | solution.py:228
  13.2 0.0 copy-done
  13.2 5.5 %collective-permute-done.1.right_ref = f32[2,4,2,8,128]{4,3,2,1,0:T(8,128)S(1)} collective-permute-done((f32[2,4,2,8,128]{4,3,2,1,0:T(8,128)S(1)}, f32[2,4,2,8,128]{4,3,2,1,0:T(8,128)S(1)}, u32[]{:S(2)}, u32[]{:S(2)}) %collective-permute-start.1) | collective-permute-done | bytes 65568 | tf_op jit(solution)/shard_map/ppermute | solution.py:228
  18.7 0.0 copy-start.3
  18.7 0.6 %copy-done.3 = f32[2,4,2,8,128]{4,3,2,1,0:T(8,128)} copy-done((f32[2,4,2,8,128]{4,3,2,1,0:T(8,128)}, f32[2,4,2,8,128]{4,3,2,1,0:T(8,128)S(1)}, u32[]{:S(2)}) %copy-start.3) | copy-done | bytes 65560
  19.4 9.9 %density.1.rho_ref = f32[8,128]{1,0:T(8,128)} custom-call(f32[2,2,2,8,128]{4,3,2,1,0:T(8,128)} %copy-done, f32[2,2,2,8,128]{4,3,2,1,0:T(8,128)} %copy-done.2, f32[2,4,2,8,128]{4,3,2,1,0:T(8,128)} %copy-done.3), custom_call_target="tpu_custom_call" | custom-call | tf_op jit(solution)/shard_map/density/pallas_call | solution.py:238
  29.3 0.0 copy-start.4
  29.3 0.7 %slice_bitcast_fusion.1 = f32[2,8,128]{2,1,0:T(8,128)S(1)} fusion(f32[2,4,2,8,128]{4,3,2,1,0:T(8,128)} %copy-done.3), kind=kLoop, calls=%fused_computation.9 | loop fusion | bytes 16384 | tf_op jit(solution)/shard_map/squeeze | solution.py:250
  30.0 0.0 copy-start.1
  30.0 0.0 copy-done.4
  30.0 0.1 collective-permute-start.2
  30.1 0.7 %copy-done.1 = f32[2,2,2,8,128]{4,3,2,1,0:T(8,128)S(1)} copy-done((f32[2,2,2,8,128]{4,3,2,1,0:T(8,128)S(1)}, f32[2,2,2,8,128]{4,3,2,1,0:T(8,128)}, u32[]{:S(2)}) %copy-start.1) | copy-done | bytes 32792
  30.8 6.8 %collective-permute-done.2.down_ref = f32[7,8,128]{2,1,0:T(8,128)S(1)} collective-permute-done((f32[7,8,128]{2,1,0:T(8,128)S(1)}, f32[7,8,128]{2,1,0:T(8,128)S(1)}, u32[]{:S(2)}, u32[]{:S(2)}) %collective-permute-start.2) | collective-permute-done | bytes 28704 | tf_op jit(solution)/shard_map/ppermute | solution.py:228
  37.6 0.0 copy-start.5
  37.6 0.7 %constant_dynamic-update-slice_fusion.2 = f32[10,8,128]{2,1,0:T(8,128)S(1)} fusion(f32[10,8,128]{2,1,0:T(8,128)S(1)} %constant_dynamic-update-slice_fusion.3, f32[2,2,2,8,128]{4,3,2,1,0:T(8,128)} %copy-done.2), kind=kLoop, calls=%fused_computation.5 | loop fusion | bytes 16384
  38.3 0.0 copy-done.5
  38.3 0.0 collective-permute-start.3
  38.3 4.0 %collective-permute-done.3.left_ref = f32[10,8,128]{2,1,0:T(8,128)S(1)} collective-permute-done((f32[10,8,128]{2,1,0:T(8,128)S(1)}, f32[10,8,128]{2,1,0:T(8,128)S(1)}, u32[]{:S(2)}, u32[]{:S(2)}) %collective-permute-start.3) | collective-permute-done | bytes 40992 | tf_op jit(solution)/shard_map/ppermute | solution.py:228
  42.3 0.0 copy-start.6
  42.3 0.6 %copy-done.6 = f32[10,8,128]{2,1,0:T(8,128)} copy-done((f32[10,8,128]{2,1,0:T(8,128)}, f32[10,8,128]{2,1,0:T(8,128)S(1)}, u32[]{:S(2)}) %copy-start.6) | copy-done | bytes 40984
  43.0 17.3 %force.1 = (f32[2,2,2,128]{3,2,1,0:T(2,128)}, f32[3,2,2,2,128]{4,3,2,1,0:T(2,128)}, f32[2,2,2,128]{3,2,1,0:T(2,128)}) custom-call(f32[2,2,2,8,128]{4,3,2,1,0:T(8,128)} %copy-done, f32[2,2,2,8,128]{4,3,2,1,0:T(8,128)} %copy-done.2, f32[2,4,2,8,128]{4,3,2,1,0:T(8,128)} %copy-done.3, f32[8,128]{1,0:T(8,128)} %density.1.rho_ref, f32[7,8,128]{2,1,0:T(8,128)} %copy-done.5, ...), custom_call_target="tpu_custom_call" | custom-call | tf_op jit(solution)/shard_map/force/pallas_call | solution.py:254
  (10 shorter events, 0.0 us)
Async XLA Ops:
  0.6 0.7 %copy-start.7 = (f32[3,2,2,2,128]{4,3,2,1,0:T(2,128)S(1)}, f32[3,2,2,2,128]{4,3,2,1,0:T(2,128)}, u32[]{:S(2)}) copy-start(f32[3,2,2,2,128]{4,3,2,1,0:T(2,128)} %param.6) | copy-start | bytes 36868
  1.4 0.7 %copy-start.9 = (f32[2,2,2,128]{3,2,1,0:T(2,128)S(1)}, f32[2,2,2,128]{3,2,1,0:T(2,128)}, u32[]{:S(2)}) copy-start(f32[2,2,2,128]{3,2,1,0:T(2,128)} %param.7) | copy-start | bytes 12292
  1.4 0.7 %copy-start.10 = (s32[2,2,2]{2,1,0:T(2,128)S(1)}, s32[2,2,2]{2,1,0:T(2,128)}, u32[]{:S(2)}) copy-start(s32[2,2,2]{2,1,0:T(2,128)} %param.9) | copy-start | bytes 100
  2.1 0.7 %copy-start.8 = (f32[2,2,2,128]{3,2,1,0:T(2,128)S(1)}, f32[2,2,2,128]{3,2,1,0:T(2,128)}, u32[]{:S(2)}) copy-start(f32[2,2,2,128]{3,2,1,0:T(2,128)} %param.8) | copy-start | bytes 12292
  2.8 10.4 %copy-start = (f32[2,2,2,8,128]{4,3,2,1,0:T(8,128)}, f32[2,2,2,8,128]{4,3,2,1,0:T(8,128)S(1)}, u32[]{:S(2)}) copy-start(f32[2,2,2,8,128]{4,3,2,1,0:T(8,128)S(1)} %maximum_bitcast_fusion.own_ref) | copy-start | bytes 98308
  2.8 9.0 %collective-permute-start = (f32[2,2,2,8,128]{4,3,2,1,0:T(8,128)S(1)}, f32[2,2,2,8,128]{4,3,2,1,0:T(8,128)S(1)}, u32[]{:S(2)}, u32[]{:S(2)}) collective-permute-start(f32[2,2,2,8,128]{4,3,2,1,0:T(8,128)S(1)} %maximum_bitcast_fusion.own_ref), channel_id=1, source_target_pairs={{1,0},{2,1},{3,2},{4,3},{5,4},{6,5},{7,6},{8,7},{9,8},{10,9},{11,1... | collective-permute-start | bytes 98312 | tf_op jit(solution)/shard_map/ppermute | solution.py:228
  11.7 0.6 %copy-start.2 = (f32[2,2,2,8,128]{4,3,2,1,0:T(8,128)}, f32[2,2,2,8,128]{4,3,2,1,0:T(8,128)S(1)}, u32[]{:S(2)}) copy-start(f32[2,2,2,8,128]{4,3,2,1,0:T(8,128)S(1)} %collective-permute-done.up_ref) | copy-start | bytes 98308
  12.4 6.4 %collective-permute-start.1 = (f32[2,4,2,8,128]{4,3,2,1,0:T(8,128)S(1)}, f32[2,4,2,8,128]{4,3,2,1,0:T(8,128)S(1)}, u32[]{:S(2)}, u32[]{:S(2)}) collective-permute-start(f32[2,4,2,8,128]{4,3,2,1,0:T(8,128)S(1)} %pad_maximum_fusion), channel_id=1, source_target_pairs={{32,0},{64,32},{96,64},{128,96},{160,128},{192,160},{224,192},{0,2... | collective-permute-start | bytes 196616 | tf_op jit(solution)/shard_map/ppermute | solution.py:228
  18.7 0.6 %copy-start.3 = (f32[2,4,2,8,128]{4,3,2,1,0:T(8,128)}, f32[2,4,2,8,128]{4,3,2,1,0:T(8,128)S(1)}, u32[]{:S(2)}) copy-start(f32[2,4,2,8,128]{4,3,2,1,0:T(8,128)S(1)} %collective-permute-done.1.right_ref) | copy-start | bytes 196612
  29.3 0.7 %copy-start.4 = (f32[8,128]{1,0:T(8,128)S(1)}, f32[8,128]{1,0:T(8,128)}, u32[]{:S(2)}) copy-start(f32[8,128]{1,0:T(8,128)} %density.1.rho_ref) | copy-start | bytes 12292
  30.0 0.8 %copy-start.1 = (f32[2,2,2,8,128]{4,3,2,1,0:T(8,128)S(1)}, f32[2,2,2,8,128]{4,3,2,1,0:T(8,128)}, u32[]{:S(2)}) copy-start(f32[2,2,2,8,128]{4,3,2,1,0:T(8,128)} %copy-done) | copy-start | bytes 98308
  30.0 7.6 %collective-permute-start.2 = (f32[7,8,128]{2,1,0:T(8,128)S(1)}, f32[7,8,128]{2,1,0:T(8,128)S(1)}, u32[]{:S(2)}, u32[]{:S(2)}) collective-permute-start(f32[7,8,128]{2,1,0:T(8,128)S(1)} %pad_maximum_fusion.1), channel_id=1, source_target_pairs={{31,0},{0,1},{1,2},{2,3},{3,4},{4,5},{5,6},{6,7},{7,8},{8,9},{9,10... | collective-permute-start | bytes 86024 | tf_op jit(solution)/shard_map/ppermute | solution.py:228
  37.6 0.7 %copy-start.5 = (f32[7,8,128]{2,1,0:T(8,128)}, f32[7,8,128]{2,1,0:T(8,128)S(1)}, u32[]{:S(2)}) copy-start(f32[7,8,128]{2,1,0:T(8,128)S(1)} %collective-permute-done.2.down_ref) | copy-start | bytes 86020
  38.3 4.0 %collective-permute-start.3 = (f32[10,8,128]{2,1,0:T(8,128)S(1)}, f32[10,8,128]{2,1,0:T(8,128)S(1)}, u32[]{:S(2)}, u32[]{:S(2)}) collective-permute-start(f32[10,8,128]{2,1,0:T(8,128)S(1)} %constant_dynamic-update-slice_fusion), channel_id=1, source_target_pairs={{224,0},{0,32},{32,64},{64,96},{96,128},{128,160},{160,192},{192,2... | collective-permute-start | bytes 122888 | tf_op jit(solution)/shard_map/ppermute | solution.py:228
  42.3 0.6 %copy-start.6 = (f32[10,8,128]{2,1,0:T(8,128)}, f32[10,8,128]{2,1,0:T(8,128)S(1)}, u32[]{:S(2)}) copy-start(f32[10,8,128]{2,1,0:T(8,128)S(1)} %collective-permute-done.3.left_ref) | copy-start | bytes 122884
